TPU v7x, 32 devices: a whole 2x2x4 slice. The times are simulated.
32 devices in a mesh: fsdp: 2 (over x), context: 4 (over y, core), tensor: 4 (over z).
Axes of the slice: x: 2, y: 2, z: 4, core: 2. Of those that a mesh axis runs over, the one named last changes fastest.
Arguments:
- hidden_in: bfloat16 [2, 1024, 2048], P('fsdp', ('context', 'tensor')), may hold values from -6 to 6
- segment_ids: int32 [2, 1024], P('fsdp'), may hold values from 0 to 15, never falling along the last dimension, each value on 1 to 512 neighbouring positions
- pad_mask: int32 [2, 1024], P('fsdp'), may hold values from 0 to 1, as said below
- attn_gain: bfloat16 [2048], P(('fsdp', 'context')), may hold values from 0.5 to 1.5
- w_query: bfloat16 [2048, 2048], P(('fsdp', 'context'), 'tensor'), may hold values from -0.1875 to 0.1875
- w_key: bfloat16 [2048, 256], P(('fsdp', 'context'), 'tensor'), may hold values from -0.1875 to 0.1875
- w_value: bfloat16 [2048, 256], P(('fsdp', 'context'), 'tensor'), may hold values from -0.125 to 0.125
- w_out: bfloat16 [2048, 2048], P('tensor', ('fsdp', 'context')), may hold values from -0.5 to 0.5
- mlp_gain: bfloat16 [2048], P(('fsdp', 'context')), may hold values from 0.5 to 1.5
- w_gate: bfloat16 [2048, 5632], P(('fsdp', 'context'), 'tensor'), may hold values from -0.125 to 0.125
- w_up: bfloat16 [2048, 5632], P(('fsdp', 'context'), 'tensor'), may hold values from -0.125 to 0.125
- w_down: bfloat16 [5632, 2048], P('tensor', ('fsdp', 'context')), may hold values from -0.078125 to 0.078125
- cotangent: bfloat16 [2, 1024, 2048], P('fsdp', ('context', 'tensor')), may hold values from -6 to 6
Outputs:
- block_out: bfloat16 [2, 1024, 2048], P('fsdp', ('context', 'tensor'))
- grad_hidden: float32 [2, 1024, 2048], P('fsdp', ('context', 'tensor'))
- grad_attn_gain: float32 [2048], P(('fsdp', 'context'))
- grad_query: float32 [2048, 2048], P(('fsdp', 'context'), 'tensor')
- grad_key: float32 [2048, 256], P(('fsdp', 'context'), 'tensor')
- grad_value: float32 [2048, 256], P(('fsdp', 'context'), 'tensor')
- grad_out: float32 [2048, 2048], P('tensor', ('fsdp', 'context'))
- grad_mlp_gain: float32 [2048], P(('fsdp', 'context'))
- grad_gate: float32 [2048, 5632], P(('fsdp', 'context'), 'tensor')
- grad_up: float32 [2048, 5632], P(('fsdp', 'context'), 'tensor')
- grad_down: float32 [5632, 2048], P('tensor', ('fsdp', 'context'))
Inputs may be any that keep to these rules, and one draw needn't show every extreme that they name: `segment_ids`: ids never fall along a sequence; a document is a run of 1 to 512 consecutive tokens of one id. `pad_mask`: every sequence ends in one or more padding slots, and no other slot is padding.
All inputs are finite; a program needn't handle non-finite values.
Results may differ from a plain program's by a relative error of at most 0.013.
The roundings to bfloat16 on the way count: a program that leaves them out, or rounds other values in their place, can miss the bound.
Values may be sent and summed in bfloat16 or wider, within the bound.
A program may use at most 88 MiB of HBM per device.

v0:
```python
import math
import jax
import jax.numpy as jnp
from jax import lax
from jax.sharding import PartitionSpec as P

EPS = 1e-05
NEG = -1e30


def positions_of(segments):
    length = segments.shape[1]
    columns = jnp.arange(length, dtype=jnp.int32)[None, :]
    previous = jnp.concatenate(
        [jnp.full((segments.shape[0], 1), -1, jnp.int32), segments[:, :-1]], axis=1
    )
    starts = jnp.where(segments != previous, columns, jnp.zeros_like(columns))
    return columns - lax.cummax(starts, axis=1)


def rope_tables(positions, head_size):
    half_size = head_size // 2
    frequency = jnp.exp(
        -(jnp.arange(half_size, dtype=jnp.float32) * (2.0 / head_size)) * math.log(10000.0)
    )
    angles = positions.astype(jnp.float32)[..., None] * frequency
    return (jnp.cos(angles)[..., None, :], jnp.sin(angles)[..., None, :])


def rotate(vectors, cos_table, sin_table):
    half_size = vectors.shape[-1] // 2
    first_half = vectors[..., :half_size]
    second_half = vectors[..., half_size:]
    return jnp.concatenate(
        [
            first_half * cos_table - second_half * sin_table,
            second_half * cos_table + first_half * sin_table,
        ],
        axis=-1,
    )


def allowed_of(seg_row, pad_row):
    length = seg_row.shape[0]
    columns = jnp.arange(length, dtype=jnp.int32)
    same_doc = seg_row[:, None] == seg_row[None, :]
    causal = columns[None, :] <= columns[:, None]
    live_key = (pad_row[None, :] == 1) | (columns[:, None] == columns[None, :])
    return same_doc & causal & live_key


def matmul(left_side, right_side):
    return jnp.dot(left_side, right_side, preferred_element_type=jnp.float32)


def matmul_left_t(left_side, right_side):
    return lax.dot_general(
        left_side, right_side, (((0,), (0,)), ((), ())), preferred_element_type=jnp.float32
    )


def matmul_right_t(left_side, right_side):
    return lax.dot_general(
        left_side, right_side, (((1,), (1,)), ((), ())), preferred_element_type=jnp.float32
    )


def rows_gather(activations):
    return lax.all_gather(activations, "tensor", axis=1, tiled=True)


def rows_sum(partials):
    return lax.psum_scatter(partials, "tensor", scatter_dimension=1, tiled=True)


def to_heads(by_rows):
    return lax.all_to_all(by_rows, "context", split_axis=2, concat_axis=1, tiled=True)


def to_spans(by_heads):
    return lax.all_to_all(by_heads, "context", split_axis=1, concat_axis=2, tiled=True)


def norm_back(grad_normed, vectors, inv_scale, gain_row):
    unit_rows = vectors * inv_scale
    weighted = grad_normed * gain_row.astype(jnp.float32)
    grad_gain = jnp.sum(grad_normed * unit_rows, axis=(0, 1))
    grad_vectors = inv_scale * (
        weighted - unit_rows * jnp.mean(weighted * unit_rows, axis=-1, keepdims=True)
    )
    return (grad_vectors, grad_gain)


def attend_scores(query_rows, kv_rows, seg_row, pad_row):
    length = query_rows.shape[0]
    head_size = kv_rows.shape[1] // 2
    query_heads = query_rows.reshape(length, -1, head_size)
    key_rows = kv_rows[:, :head_size]
    value_rows = kv_rows[:, head_size:]
    scores = jnp.einsum(
        "qhd,td->hqt", query_heads, key_rows, preferred_element_type=jnp.float32
    ) * head_size ** (-0.5)
    scores = jnp.where(allowed_of(seg_row, pad_row)[None], scores, NEG)
    return (query_heads, key_rows, value_rows, scores)


def attend_forward(packed_item):
    query_rows, kv_rows, seg_row, pad_row = packed_item
    query_heads, key_rows, value_rows, scores = attend_scores(query_rows, kv_rows, seg_row, pad_row)
    row_max = jnp.max(scores, axis=-1, keepdims=True)
    exp_scores = jnp.exp(scores - row_max)
    row_total = jnp.sum(exp_scores, axis=-1, keepdims=True)
    weights = exp_scores / row_total
    output = jnp.einsum(
        "hqt,td->qhd", weights.astype(jnp.bfloat16), value_rows, preferred_element_type=jnp.float32
    )
    output = output.reshape(query_rows.shape[0], -1).astype(jnp.bfloat16)
    return (output, (row_max + jnp.log(row_total))[..., 0])


def attend_backward(packed_item):
    query_rows, kv_rows, grad_rows, log_total, seg_row, pad_row = packed_item
    query_heads, key_rows, value_rows, scores = attend_scores(query_rows, kv_rows, seg_row, pad_row)
    head_size = key_rows.shape[1]
    scale = head_size ** (-0.5)
    weights = jnp.exp(scores - log_total[..., None])
    grad_heads = grad_rows.reshape(query_heads.shape)
    grad_weights = jnp.einsum(
        "qhd,td->hqt", grad_heads, value_rows, preferred_element_type=jnp.float32
    )
    row_delta = jnp.sum(weights * grad_weights, axis=-1, keepdims=True)
    grad_scores = (weights * (grad_weights - row_delta)).astype(jnp.bfloat16)
    grad_queries = (
        jnp.einsum("hqt,td->qhd", grad_scores, key_rows, preferred_element_type=jnp.float32) * scale
    )
    grad_keys = (
        jnp.einsum("hqt,qhd->td", grad_scores, query_heads, preferred_element_type=jnp.float32)
        * scale
    )
    grad_values = jnp.einsum(
        "hqt,qhd->td", weights.astype(jnp.bfloat16), grad_heads, preferred_element_type=jnp.float32
    )
    return (grad_queries, jnp.concatenate([grad_keys, grad_values], axis=-1))


def forward_pass(params, tables):
    hidden_in, attn_gain, w_query, w_key, w_value, w_out, mlp_gain, w_gate, w_up, w_down = params
    cos_span, sin_span, segment_ids, pad_mask, keep_rows = tables
    gain_one, query_all, key_all, value_all, out_all = (
        lax.all_gather(attn_gain, ("fsdp", "context"), axis=0, tiled=True),
        lax.all_gather(w_query, ("fsdp", "context"), axis=0, tiled=True),
        lax.all_gather(w_key, ("fsdp", "context"), axis=0, tiled=True),
        lax.all_gather(w_value, ("fsdp", "context"), axis=0, tiled=True),
        lax.all_gather(w_out, ("fsdp", "context"), axis=1, tiled=True),
    )
    seq_count, row_count, model_width = hidden_in.shape
    head_size = key_all.shape[1]
    hidden_f = hidden_in.astype(jnp.float32)
    scale_one = lax.rsqrt(jnp.mean(hidden_f * hidden_f, axis=-1, keepdims=True) + EPS)
    normed_one = rows_gather(
        (hidden_f * scale_one * gain_one.astype(jnp.float32)).astype(jnp.bfloat16)
    )
    span_len = normed_one.shape[1]
    flat_one = normed_one.reshape(-1, model_width)
    query_pre = matmul(flat_one, query_all).reshape(seq_count, span_len, -1, head_size)
    queries = (
        rotate(query_pre, cos_span, sin_span).astype(jnp.bfloat16).reshape(seq_count, span_len, -1)
    )
    key_pre = matmul(flat_one, key_all).reshape(seq_count, span_len, 1, head_size)
    key_rows = (
        rotate(key_pre, cos_span, sin_span)
        .astype(jnp.bfloat16)
        .reshape(seq_count, span_len, head_size)
    )
    value_rows = (
        matmul(flat_one, value_all).astype(jnp.bfloat16).reshape(seq_count, span_len, head_size)
    )
    query_full = to_heads(queries)
    kv_full = lax.all_gather(
        jnp.concatenate([key_rows, value_rows], axis=-1), "context", axis=1, tiled=True
    )
    attn_full, log_total = lax.map(attend_forward, (query_full, kv_full, segment_ids, pad_mask))
    out_span = to_spans(attn_full)
    out_flat = out_span.reshape(-1, out_span.shape[2])
    branch_one = rows_sum(matmul(out_flat, out_all).reshape(seq_count, span_len, model_width))
    middle = hidden_f + branch_one
    gain_two, gate_all, up_all, down_all = (
        lax.all_gather(mlp_gain, ("fsdp", "context"), axis=0, tiled=True),
        lax.all_gather(w_gate, ("fsdp", "context"), axis=0, tiled=True),
        lax.all_gather(w_up, ("fsdp", "context"), axis=0, tiled=True),
        lax.all_gather(w_down, ("fsdp", "context"), axis=1, tiled=True),
    )
    scale_two = lax.rsqrt(jnp.mean(middle * middle, axis=-1, keepdims=True) + EPS)
    normed_two = rows_gather(
        (middle * scale_two * gain_two.astype(jnp.float32)).astype(jnp.bfloat16)
    )
    flat_two = normed_two.reshape(-1, model_width)
    gate_rows = matmul(flat_two, gate_all)
    up_rows = matmul(flat_two, up_all)
    inner_rows = (jax.nn.silu(gate_rows) * up_rows).astype(jnp.bfloat16)
    branch_two = rows_sum(matmul(inner_rows, down_all).reshape(seq_count, span_len, model_width))
    block_out = (keep_rows * (middle + branch_two)).astype(jnp.bfloat16)
    return dict(
        block_out=block_out,
        gain_one=gain_one,
        query_all=query_all,
        key_all=key_all,
        value_all=value_all,
        out_all=out_all,
        gain_two=gain_two,
        gate_all=gate_all,
        up_all=up_all,
        down_all=down_all,
        hidden_f=hidden_f,
        scale_one=scale_one,
        flat_one=flat_one,
        query_full=query_full,
        kv_full=kv_full,
        log_total=log_total,
        out_flat=out_flat,
        middle=middle,
        scale_two=scale_two,
        flat_two=flat_two,
        gate_rows=gate_rows,
        up_rows=up_rows,
        inner_rows=inner_rows,
    )


def body(
    hidden_in,
    segment_ids,
    pad_mask,
    attn_gain,
    w_query,
    w_key,
    w_value,
    w_out,
    mlp_gain,
    w_gate,
    w_up,
    w_down,
    cotangent,
):
    seq_count, row_count, model_width = hidden_in.shape
    context_count = lax.axis_size("context")
    tensor_count = lax.axis_size("tensor")
    context_index = lax.axis_index("context")
    tensor_index = lax.axis_index("tensor")
    seq_length = segment_ids.shape[1]
    span_len = seq_length // context_count
    head_size = w_key.shape[1]
    cos_full, sin_full = rope_tables(positions_of(segment_ids), head_size)
    cos_span = lax.dynamic_slice_in_dim(cos_full, context_index * span_len, span_len, 1)
    sin_span = lax.dynamic_slice_in_dim(sin_full, context_index * span_len, span_len, 1)
    row_start = (context_index * tensor_count + tensor_index) * row_count
    keep_rows = lax.dynamic_slice_in_dim(pad_mask, row_start, row_count, 1).astype(jnp.float32)[
        ..., None
    ]
    tables = (cos_span, sin_span, segment_ids, pad_mask, keep_rows)
    params = (hidden_in, attn_gain, w_query, w_key, w_value, w_out, mlp_gain, w_gate, w_up, w_down)
    first_pass = forward_pass(params, tables)
    saved_state = forward_pass(lax.optimization_barrier(params), tables)
    grad_rows = cotangent.astype(jnp.float32) * keep_rows
    grad_down_in = rows_gather(grad_rows.astype(jnp.bfloat16)).reshape(-1, model_width)
    grad_down = matmul_left_t(saved_state["inner_rows"], grad_down_in)
    grad_inner = matmul_right_t(grad_down_in, saved_state["down_all"])
    gate_rows = saved_state["gate_rows"]
    sigmoid_gate = jax.nn.sigmoid(gate_rows)
    grad_gate_rows = (
        grad_inner
        * saved_state["up_rows"]
        * sigmoid_gate
        * (1.0 + gate_rows * (1.0 - sigmoid_gate))
    ).astype(jnp.bfloat16)
    grad_up_rows = (grad_inner * gate_rows * sigmoid_gate).astype(jnp.bfloat16)
    grad_gate = matmul_left_t(saved_state["flat_two"], grad_gate_rows)
    grad_up = matmul_left_t(saved_state["flat_two"], grad_up_rows)
    grad_gate, grad_up, grad_down = (
        lax.psum_scatter(grad_gate, ("fsdp", "context"), scatter_dimension=0, tiled=True),
        lax.psum_scatter(grad_up, ("fsdp", "context"), scatter_dimension=0, tiled=True),
        lax.psum_scatter(grad_down, ("fsdp", "context"), scatter_dimension=1, tiled=True),
    )
    grad_normed_two = matmul_right_t(grad_gate_rows, saved_state["gate_all"]) + matmul_right_t(
        grad_up_rows, saved_state["up_all"]
    )
    grad_normed_two = rows_sum(grad_normed_two.reshape(seq_count, span_len, model_width))
    grad_middle_norm, grad_gain_two = norm_back(
        grad_normed_two, saved_state["middle"], saved_state["scale_two"], saved_state["gain_two"]
    )
    grad_middle = grad_rows + grad_middle_norm
    grad_attn_in = rows_gather(grad_middle.astype(jnp.bfloat16)).reshape(-1, model_width)
    grad_out = matmul_left_t(saved_state["out_flat"], grad_attn_in)
    grad_attn_rows = matmul_right_t(grad_attn_in, saved_state["out_all"]).astype(jnp.bfloat16)
    grad_heads = to_heads(grad_attn_rows.reshape(seq_count, span_len, -1))
    grad_query_full, grad_kv_full = lax.map(
        attend_backward,
        (
            saved_state["query_full"],
            saved_state["kv_full"],
            grad_heads,
            saved_state["log_total"],
            segment_ids,
            pad_mask,
        ),
    )
    grad_query_full = (
        rotate(grad_query_full, cos_full, -sin_full)
        .astype(jnp.bfloat16)
        .reshape(seq_count, seq_length, -1)
    )
    grad_query_rows = to_spans(grad_query_full).reshape(seq_count * span_len, -1)
    grad_kv_span = lax.psum_scatter(grad_kv_full, "context", scatter_dimension=1, tiled=True)
    grad_key_rows = rotate(
        grad_kv_span[..., :head_size].reshape(seq_count, span_len, 1, head_size),
        cos_span,
        -sin_span,
    )
    grad_key_rows = grad_key_rows.astype(jnp.bfloat16).reshape(-1, head_size)
    grad_value_rows = grad_kv_span[..., head_size:].astype(jnp.bfloat16).reshape(-1, head_size)
    flat_one = saved_state["flat_one"]
    grad_query = matmul_left_t(flat_one, grad_query_rows)
    grad_key = matmul_left_t(flat_one, grad_key_rows)
    grad_value = matmul_left_t(flat_one, grad_value_rows)
    grad_normed_one = (
        matmul_right_t(grad_query_rows, saved_state["query_all"])
        + matmul_right_t(grad_key_rows, saved_state["key_all"])
        + matmul_right_t(grad_value_rows, saved_state["value_all"])
    )
    grad_normed_one = rows_sum(grad_normed_one.reshape(seq_count, span_len, model_width))
    grad_input_norm, grad_gain_one = norm_back(
        grad_normed_one, saved_state["hidden_f"], saved_state["scale_one"], saved_state["gain_one"]
    )
    grad_hidden = grad_middle + grad_input_norm
    grad_gain_one, grad_gain_two = lax.psum((grad_gain_one, grad_gain_two), "tensor")
    grad_gain_one, grad_query, grad_key, grad_value, grad_out, grad_gain_two = (
        lax.psum_scatter(grad_gain_one, ("fsdp", "context"), scatter_dimension=0, tiled=True),
        lax.psum_scatter(grad_query, ("fsdp", "context"), scatter_dimension=0, tiled=True),
        lax.psum_scatter(grad_key, ("fsdp", "context"), scatter_dimension=0, tiled=True),
        lax.psum_scatter(grad_value, ("fsdp", "context"), scatter_dimension=0, tiled=True),
        lax.psum_scatter(grad_out, ("fsdp", "context"), scatter_dimension=1, tiled=True),
        lax.psum_scatter(grad_gain_two, ("fsdp", "context"), scatter_dimension=0, tiled=True),
    )
    return (
        first_pass["block_out"],
        grad_hidden,
        grad_gain_one,
        grad_query,
        grad_key,
        grad_value,
        grad_out,
        grad_gain_two,
        grad_gate,
        grad_up,
        grad_down,
    )


def solution(mesh):
    in_specs = (
        P("fsdp", ("context", "tensor"), None),
        P("fsdp", None),
        P("fsdp", None),
        P(("fsdp", "context")),
        P(("fsdp", "context"), "tensor"),
        P(("fsdp", "context"), "tensor"),
        P(("fsdp", "context"), "tensor"),
        P("tensor", ("fsdp", "context")),
        P(("fsdp", "context")),
        P(("fsdp", "context"), "tensor"),
        P(("fsdp", "context"), "tensor"),
        P("tensor", ("fsdp", "context")),
        P("fsdp", ("context", "tensor"), None),
    )
    out_specs = (
        P("fsdp", ("context", "tensor"), None),
        P("fsdp", ("context", "tensor"), None),
        P(("fsdp", "context")),
        P(("fsdp", "context"), "tensor"),
        P(("fsdp", "context"), "tensor"),
        P(("fsdp", "context"), "tensor"),
        P("tensor", ("fsdp", "context")),
        P(("fsdp", "context")),
        P(("fsdp", "context"), "tensor"),
        P(("fsdp", "context"), "tensor"),
        P("tensor", ("fsdp", "context")),
    )
    return jax.shard_map(body, mesh=mesh, in_specs=in_specs, out_specs=out_specs, check_vma=False)
```

profile of v0, /device:TPU:0, one launch (start us, length us, event | category | flops | bytes accessed | tf_op | source)
XLA Modules:
  0.0 1386.3 jit_solution(9212681209821931771)
XLA Ops:
  9.0 10.3 all-gather.2
  23.4 8.8 all-gather
  37.4 9.1 all_gather.92
  46.5 9.6 all_gather.93
  65.9 13.0 all-gather.37.cloned.1.call-done
  82.9 25.8 %all-gather.23.cloned.1.call-done = bf16[2048,512]{1,0:T(8,128)(2,1)} async-done(((bf16[256,512]{1,0:T(8,128)(2,1)}), bf16[2048,512]{1,0:T(8,128)(2,1)}) %all-gather.23.cloned.1.call-update) | async-done | bytes 2097168 | tf_op jit(solution)/shard_map/all_gather | solution.py:151
  114.8 23.8 %all-gather.21.cloned.1.call-done = bf16[1,256,2048]{2,1,0:T(8,128)(2,1)} async-done(((bf16[1,64,2048]{2,1,0:T(8,128)(2,1)}), bf16[1,256,2048]{2,1,0:T(8,128)(2,1)}) %all-gather.21.cloned.1.call-update) | async-done | bytes 1048592 | tf_op jit(solution)/shard_map/all_gather | solution.py:69
  148.4 9.6 all_gather.94
  169.3 8.4 all_to_all.90
  182.1 8.8 all-gather.3
  191.0 35.0 %reduce-scatter.18.cloned.1.call-done = f32[1,64,2048]{2,1,0:T(8,128)} async-done(((f32[1,256,2048]{2,1,0:T(8,128)}), f32[1,64,2048]{2,1,0:T(8,128)}) %reduce-scatter.18.cloned.1.call-update) | async-done | bytes 524304 | tf_op jit(solution)/shard_map/reduce_scatter | solution.py:73
  233.9 22.6 %all-gather.45.cloned.1.call-done = bf16[1,256,2048]{2,1,0:T(8,128)(2,1)} async-done(((bf16[1,64,2048]{2,1,0:T(8,128)(2,1)}), bf16[1,256,2048]{2,1,0:T(8,128)(2,1)}) %all-gather.45.cloned.1.call-update) | async-done | bytes 1048592 | tf_op jit(solution)/shard_map/all_gather | solution.py:69
  256.5 44.9 %all-gather.47.cloned.1.call-done = bf16[2048,1408]{1,0:T(8,128)(2,1)} async-done(((bf16[256,1408]{1,0:T(8,128)(2,1)}), bf16[2048,1408]{1,0:T(8,128)(2,1)}) %all-gather.47.cloned.1.call-update) | async-done | bytes 5767184 | tf_op jit(solution)/shard_map/all_gather | solution.py:190
  301.4 5.9 fusion.40
  307.3 39.5 %all-gather.49.cloned.1.call-done = bf16[2048,1408]{1,0:T(8,128)(2,1)} async-done(((bf16[256,1408]{1,0:T(8,128)(2,1)}), bf16[2048,1408]{1,0:T(8,128)(2,1)}) %all-gather.49.cloned.1.call-update) | async-done | bytes 5767184 | tf_op jit(solution)/shard_map/all_gather | solution.py:189
  352.3 24.5 %all-gather.41.cloned.1.call-done = bf16[1,256,2048]{2,1,0:T(8,128)(2,1)} async-done(((bf16[1,64,2048]{2,1,0:T(8,128)(2,1)}), bf16[1,256,2048]{2,1,0:T(8,128)(2,1)}) %all-gather.41.cloned.1.call-update) | async-done | bytes 1048592 | tf_op jit(solution)/shard_map/all_gather | solution.py:69
  376.8 45.9 %all-gather.43.cloned.1.call-done = bf16[1408,2048]{1,0:T(8,128)(2,1)} async-done(((bf16[1408,256]{1,0:T(8,128)(2,1)}), bf16[1408,2048]{1,0:T(8,128)(2,1)}) %all-gather.43.cloned.1.call-update) | async-done | bytes 5767184 | tf_op jit(solution)/shard_map/all_gather | solution.py:191
  422.7 6.1 multiply_convert_fusion.1
  436.7 44.0 %reduce-scatter.20.cloned.1.call-done = f32[1,64,2048]{2,1,0:T(8,128)} async-done(((f32[1,256,2048]{2,1,0:T(8,128)}), f32[1,64,2048]{2,1,0:T(8,128)}) %reduce-scatter.20.cloned.1.call-update) | async-done | bytes 524304 | tf_op jit(solution)/shard_map/reduce_scatter | solution.py:73
  484.6 27.4 %all-gather.51.cloned.1.call-done = bf16[1,256,2048]{2,1,0:T(8,128)(2,1)} async-done(((bf16[1,64,2048]{2,1,0:T(8,128)(2,1)}), bf16[1,256,2048]{2,1,0:T(8,128)(2,1)}) %all-gather.51.cloned.1.call-update) | async-done | bytes 1048592 | tf_op jit(solution)/shard_map/all_gather | solution.py:69
  547.6 10.8 all_gather.80
  558.4 10.7 all_gather.81
  578.8 5.9 all-to-all-done
  587.1 7.3 all_gather.82
  594.4 6.5 fusion.117
  607.8 8.4 all_to_all.91
  621.1 9.3 all-gather.1
  630.5 33.1 %reduce-scatter.14.cloned.1.call-done = f32[1,64,2048]{2,1,0:T(8,128)} async-done(((f32[1,256,2048]{2,1,0:T(8,128)}), f32[1,64,2048]{2,1,0:T(8,128)}) %reduce-scatter.14.cloned.1.call-update) | async-done | bytes 524304 | tf_op jit(solution)/shard_map/reduce_scatter | solution.py:73
  680.1 10.2 all_to_all.92
  700.8 7.2 all-gather.29.cloned.1.call-done
  708.0 30.0 %all-gather.27.cloned.1.call-done = bf16[1,256,2048]{2,1,0:T(8,128)(2,1)} async-done(((bf16[1,64,2048]{2,1,0:T(8,128)(2,1)}), bf16[1,256,2048]{2,1,0:T(8,128)(2,1)}) %all-gather.27.cloned.1.call-update) | async-done | bytes 1048592 | tf_op jit(solution)/shard_map/all_gather | solution.py:69
  738.0 5.9 fusion.56
  743.9 38.8 %all-gather.31.cloned.1.call-done = bf16[2048,1408]{1,0:T(8,128)(2,1)} async-done(((bf16[256,1408]{1,0:T(8,128)(2,1)}), bf16[2048,1408]{1,0:T(8,128)(2,1)}) %all-gather.31.cloned.1.call-update) | async-done | bytes 5767184 | tf_op jit(solution)/shard_map/all_gather | solution.py:190
  782.7 46.1 %all-gather.33.cloned.1.call-done = bf16[1408,2048]{1,0:T(8,128)(2,1)} async-done(((bf16[1408,256]{1,0:T(8,128)(2,1)}), bf16[1408,2048]{1,0:T(8,128)(2,1)}) %all-gather.33.cloned.1.call-update) | async-done | bytes 5767184 | tf_op jit(solution)/shard_map/all_gather | solution.py:191
  828.8 9.5 convolution_bitcast_fusion.1
  847.7 6.1 fusion.36
  854.9 6.1 fusion.34
  862.6 7.3 fusion.42
  876.3 24.0 %all-reduce.2 = (f32[2048]{0:T(1024)S(1)}, f32[2048]{0:T(1024)S(1)}) all-reduce(f32[2048]{0:T(1024)S(1)} %get-tuple-element.99, f32[2048]{0:T(1024)S(1)} %copy-done.37), channel_id=8, replica_groups=mesh['fsdp'=2,'context'=4,'tensor'=4] {'fsdp','context'}, use_global_device_ids=true, to_apply=%region_21.22.clone | all-reduce | flops 4096 | bytes 32768
  900.5 11.3 all-reduce.3
  913.9 6.9 reduce-scatter.16.cloned.1.call-done
  922.7 35.3 %reduce-scatter.28.cloned.1.call-done = f32[256,64]{0,1:T(8,128)} async-done(((f32[2048,64]{0,1:T(8,128)}), f32[256,64]{0,1:T(8,128)}) %reduce-scatter.28.cloned.1.call-update) | async-done | bytes 65552 | tf_op jit(solution)/shard_map/reduce_scatter | solution.py:339
  958.0 38.0 %reduce-scatter.30.cloned.1.call-done = f32[256,64]{0,1:T(8,128)} async-done(((f32[2048,64]{0,1:T(8,128)}), f32[256,64]{0,1:T(8,128)}) %reduce-scatter.30.cloned.1.call-update) | async-done | bytes 65552 | tf_op jit(solution)/shard_map/reduce_scatter | solution.py:340
  996.0 55.3 %reduce-scatter.32.cloned.1.call-done = f32[512,256]{1,0:T(8,128)} async-done(((f32[512,2048]{1,0:T(8,128)}), f32[512,256]{1,0:T(8,128)}) %reduce-scatter.32.cloned.1.call-update) | async-done | bytes 524304 | tf_op jit(solution)/shard_map/reduce_scatter | solution.py:341
  1051.3 55.5 %reduce-scatter.26.cloned.1.call-done = f32[256,512]{1,0:T(8,128)} async-done(((f32[2048,512]{1,0:T(8,128)}), f32[256,512]{1,0:T(8,128)}) %reduce-scatter.26.cloned.1.call-update) | async-done | bytes 524304 | tf_op jit(solution)/shard_map/reduce_scatter | solution.py:338
  1106.8 90.7 %reduce-scatter.34.cloned.1.call-done = f32[256,1408]{1,0:T(8,128)} async-done(((f32[2048,1408]{1,0:T(8,128)}), f32[256,1408]{1,0:T(8,128)}) %reduce-scatter.34.cloned.1.call-update) | async-done | bytes 1441808 | tf_op jit(solution)/shard_map/reduce_scatter | solution.py:280
  1197.5 90.9 %reduce-scatter.36.cloned.1.call-done = f32[256,1408]{1,0:T(8,128)} async-done(((f32[2048,1408]{1,0:T(8,128)}), f32[256,1408]{1,0:T(8,128)}) %reduce-scatter.36.cloned.1.call-update) | async-done | bytes 1441808 | tf_op jit(solution)/shard_map/reduce_scatter | solution.py:281
  1288.4 90.9 %reduce-scatter.38.cloned.1.call-done = f32[1408,256]{1,0:T(8,128)} async-done(((f32[1408,2048]{1,0:T(8,128)}), f32[1408,256]{1,0:T(8,128)}) %reduce-scatter.38.cloned.1.call-update) | async-done | bytes 1441808 | tf_op jit(solution)/shard_map/reduce_scatter | solution.py:282
  (302 shorter events, 188.7 us)
Async XLA Ops:
  7.2 54.0 %all-gather.35.cloned.1.call-start = ((), (), s32[]{:S(2)}) async-start(), calls=%async_computation.28 | async-start | bytes 1310720 | tf_op jit(solution)/shard_map/all_gather | solution.py:69
  21.2 57.7 %all-gather.37.cloned.1.call-start = ((), (), s32[]{:S(2)}) async-start(), calls=%async_computation.29 | async-start | bytes 2359296 | tf_op jit(solution)/shard_map/all_gather | solution.py:151
  21.9 86.8 %all-gather.23.cloned.1.call-start = ((), (), s32[]{:S(2)}) async-start(), calls=%async_computation.20 | async-start | bytes 2359296 | tf_op jit(solution)/shard_map/all_gather | solution.py:151
  22.7 116.0 %all-gather.21.cloned.1.call-start = ((), (), s32[]{:S(2)}) async-start(), calls=%async_computation.19 | async-start | bytes 1310720 | tf_op jit(solution)/shard_map/all_gather | solution.py:69
  35.2 143.1 %all-gather.39.cloned.1.call-start = ((), (), s32[]{:S(2)}) async-start(), calls=%async_computation.30 | async-start | bytes 2359296 | tf_op jit(solution)/shard_map/all_gather | solution.py:154
  56.1 55.6 %copy-start.13 = (bf16[2048,64]{0,1:T(8,128)(2,1)}, bf16[2048,64]{0,1:T(8,128)(2,1)S(1)}, u32[]{:S(2)}) copy-start(bf16[2048,64]{0,1:T(8,128)(2,1)S(1)} %all_gather.93) | copy-start | bytes 786436
  144.9 13.1 all-to-all-start.2
  148.3 77.7 %reduce-scatter.18.cloned.1.call-start = ((), (), s32[]{:S(2)}) async-start(), calls=%async_computation.31 | async-start | bytes 2621440 | tf_op jit(solution)/shard_map/reduce_scatter | solution.py:73
  177.8 48.2 %copy-start.2 = (bf16[1,64,2048]{2,1,0:T(8,128)(2,1)S(1)}, bf16[1,64,2048]{2,1,0:T(8,128)(2,1)}, u32[]{:S(2)}) copy-start(bf16[1,64,2048]{2,1,0:T(8,128)(2,1)} %param.13) | copy-start | bytes 786436
  178.2 50.8 %copy-start.10 = (bf16[1,256,4,128]{1,3,2,0:T(8,128)(2,1)}, bf16[1,256,4,128]{1,3,2,0:T(8,128)(2,1)S(1)}, u32[]{:S(2)}) copy-start(bf16[1,256,4,128]{1,3,2,0:T(8,128)(2,1)S(1)} %copy.90) | copy-start | bytes 786436
  178.3 53.6 %copy-start.20 = (bf16[1,64,2048]{2,1,0:T(8,128)(2,1)S(1)}, bf16[1,64,2048]{2,1,0:T(8,128)(2,1)}, u32[]{:S(2)}) copy-start(bf16[1,64,2048]{2,1,0:T(8,128)(2,1)} %param.25) | copy-start | bytes 786436
  182.0 74.5 %all-gather.45.cloned.1.call-start = ((), (), s32[]{:S(2)}) async-start(), calls=%async_computation.34 | async-start | bytes 1310720 | tf_op jit(solution)/shard_map/all_gather | solution.py:69
  229.1 72.3 %all-gather.47.cloned.1.call-start = ((), (), s32[]{:S(2)}) async-start(), calls=%async_computation.35 | async-start | bytes 6488064 | tf_op jit(solution)/shard_map/all_gather | solution.py:190
  229.8 116.9 %all-gather.49.cloned.1.call-start = ((), (), s32[]{:S(2)}) async-start(), calls=%async_computation.36 | async-start | bytes 6488064 | tf_op jit(solution)/shard_map/all_gather | solution.py:189
  230.6 146.2 %all-gather.41.cloned.1.call-start = ((), (), s32[]{:S(2)}) async-start(), calls=%async_computation.32 | async-start | bytes 1310720 | tf_op jit(solution)/shard_map/all_gather | solution.py:69
  232.7 190.1 %all-gather.43.cloned.1.call-start = ((), (), s32[]{:S(2)}) async-start(), calls=%async_computation.33 | async-start | bytes 6488064 | tf_op jit(solution)/shard_map/all_gather | solution.py:191
  233.4 247.2 %reduce-scatter.20.cloned.1.call-start = ((), (), s32[]{:S(2)}) async-start(), calls=%async_computation.37 | async-start | bytes 2621440 | tf_op jit(solution)/shard_map/reduce_scatter | solution.py:73
  256.5 90.3 %copy-start.6 = (bf16[1,256,2048]{2,1,0:T(8,128)(2,1)S(1)}, bf16[1,256,2048]{2,1,0:T(8,128)(2,1)}, u32[]{:S(2)}) copy-start(bf16[1,256,2048]{2,1,0:T(8,128)(2,1)} %all-gather.45.cloned.1.call-done) | copy-start | bytes 3145732
  430.7 49.9 %copy-start.4 = (f32[1,64,2048]{2,1,0:T(8,128)S(1)}, f32[1,64,2048]{2,1,0:T(8,128)}, u32[]{:S(2)}) copy-start(f32[1,64,2048]{2,1,0:T(8,128)} %reduce-scatter.18.cloned.1.call-done) | copy-start | bytes 1572868
  430.7 49.9 %copy-start.46 = (f32[64]{0:T(128)S(1)}, f32[64]{0:T(128)}, u32[]{:S(2)}) copy-start(f32[64]{0:T(128)} %copy-done.45) | copy-start | bytes 772
  430.7 51.7 %copy-start.43 = (f32[64]{0:T(128)S(1)}, f32[64]{0:T(128)}, u32[]{:S(2)}) copy-start(f32[64]{0:T(128)} %copy-done.42) | copy-start | bytes 772
  436.6 75.5 %all-gather.51.cloned.1.call-start = ((), (), s32[]{:S(2)}) async-start(), calls=%async_computation.38 | async-start | bytes 1310720 | tf_op jit(solution)/shard_map/all_gather | solution.py:69
  482.5 39.3 %copy-start.39 = (f32[2,1024]{1,0:T(2,128)S(1)}, f32[2,1024]{1,0:T(2,128)}, u32[]{:S(2)}) copy-start(f32[2,1024]{1,0:T(2,128)} %copy-done.38) | copy-start | bytes 24580
  518.2 9.4 all-to-all-start.4
  521.6 63.9 %reduce-scatter.22.cloned.1.call-start = ((), (), s32[]{:S(2)}) async-start(), calls=%async_computation.39 | async-start | bytes 655360 | tf_op jit(solution)/shard_map/reduce_scatter | solution.py:313
  547.0 69.7 %all-gather.25.cloned.1.call-start = ((), (), s32[]{:S(2)}) async-start(), calls=%async_computation.21 | async-start | bytes 2359296 | tf_op jit(solution)/shard_map/all_gather | solution.py:154
  572.6 12.2 all-to-all-start
  576.0 87.6 %reduce-scatter.14.cloned.1.call-start = ((), (), s32[]{:S(2)}) async-start(), calls=%async_computation.22 | async-start | bytes 2621440 | tf_op jit(solution)/shard_map/reduce_scatter | solution.py:73
  620.5 47.6 %copy-start.36 = (f32[1024]{0:T(1024)S(1)}, f32[1024]{0:T(1024)}, u32[]{:S(2)}) copy-start(f32[1024]{0:T(1024)} %copy-done.35) | copy-start | bytes 12292
  620.5 47.6 %copy-start.48 = (f32[32]{0:T(128)S(1)}, f32[32]{0:T(128)}, u32[]{:S(2)}) copy-start(f32[32]{0:T(128)} %copy-done.47) | copy-start | bytes 388
  620.5 87.5 %all-gather.29.cloned.1.call-start = ((), (), s32[]{:S(2)}) async-start(), calls=%async_computation.24 | async-start | bytes 6488064 | tf_op jit(solution)/shard_map/all_gather | solution.py:189
  621.1 116.9 %all-gather.27.cloned.1.call-start = ((), (), s32[]{:S(2)}) async-start(), calls=%async_computation.23 | async-start | bytes 1310720 | tf_op jit(solution)/shard_map/all_gather | solution.py:69
  666.7 116.0 %all-gather.31.cloned.1.call-start = ((), (), s32[]{:S(2)}) async-start(), calls=%async_computation.25 | async-start | bytes 6488064 | tf_op jit(solution)/shard_map/all_gather | solution.py:190
  667.5 161.3 %all-gather.33.cloned.1.call-start = ((), (), s32[]{:S(2)}) async-start(), calls=%async_computation.26 | async-start | bytes 6488064 | tf_op jit(solution)/shard_map/all_gather | solution.py:191
  668.1 206.9 %reduce-scatter.24.cloned.1.call-start = ((), (), s32[]{:S(2)}) async-start(), calls=%async_computation.40 | async-start | bytes 2621440 | tf_op jit(solution)/shard_map/reduce_scatter | solution.py:73
  700.5 220.3 %reduce-scatter.16.cloned.1.call-start = ((), (), s32[]{:S(2)}) async-start(), calls=%async_computation.27 | async-start | bytes 2621440 | tf_op jit(solution)/shard_map/reduce_scatter | solution.py:73
  738.0 90.8 %copy-start.50 = (bf16[1,256,2048]{2,1,0:T(8,128)(2,1)S(1)}, bf16[1,256,2048]{2,1,0:T(8,128)(2,1)}, u32[]{:S(2)}) copy-start(bf16[1,256,2048]{2,1,0:T(8,128)(2,1)} %all-gather.27.cloned.1.call-done) | copy-start | bytes 3145732
  743.9 94.5 %copy-start.28 = (bf16[256,32]{0,1:T(8,128)(2,1)S(1)}, bf16[256,32]{0,1:T(8,128)(2,1)}, u32[]{:S(2)}) copy-start(bf16[256,32]{0,1:T(8,128)(2,1)} %get-tuple-element.116) | copy-start | bytes 49156
  838.3 119.7 %reduce-scatter.28.cloned.1.call-start = ((), (), s32[]{:S(2)}) async-start(), calls=%async_computation.42 | async-start | bytes 589824 | tf_op jit(solution)/shard_map/reduce_scatter | solution.py:339
  839.5 156.5 %reduce-scatter.30.cloned.1.call-start = ((), (), s32[]{:S(2)}) async-start(), calls=%async_computation.43 | async-start | bytes 589824 | tf_op jit(solution)/shard_map/reduce_scatter | solution.py:340
  840.7 210.6 %reduce-scatter.32.cloned.1.call-start = ((), (), s32[]{:S(2)}) async-start(), calls=%async_computation.44 | async-start | bytes 4718592 | tf_op jit(solution)/shard_map/reduce_scatter | solution.py:341
  843.5 263.3 %reduce-scatter.26.cloned.1.call-start = ((), (), s32[]{:S(2)}) async-start(), calls=%async_computation.41 | async-start | bytes 4718592 | tf_op jit(solution)/shard_map/reduce_scatter | solution.py:338
  846.3 351.3 %reduce-scatter.34.cloned.1.call-start = ((), (), s32[]{:S(2)}) async-start(), calls=%async_computation.45 | async-start | bytes 12976128 | tf_op jit(solution)/shard_map/reduce_scatter | solution.py:280
  853.8 434.6 %reduce-scatter.36.cloned.1.call-start = ((), (), s32[]{:S(2)}) async-start(), calls=%async_computation.46 | async-start | bytes 12976128 | tf_op jit(solution)/shard_map/reduce_scatter | solution.py:281
  861.0 518.3 %reduce-scatter.38.cloned.1.call-start = ((), (), s32[]{:S(2)}) async-start(), calls=%async_computation.47 | async-start | bytes 12976128 | tf_op jit(solution)/shard_map/reduce_scatter | solution.py:282
  869.9 41.9 %copy-start.17 = (f32[1,64,2048]{2,1,0:T(8,128)S(1)}, f32[1,64,2048]{2,1,0:T(8,128)}, u32[]{:S(2)}) copy-start(f32[1,64,2048]{2,1,0:T(8,128)} %get-tuple-element.106) | copy-start | bytes 1572868
  869.9 50.9 %copy-start.8 = (f32[1,64,2048]{2,1,0:T(8,128)S(1)}, f32[1,64,2048]{2,1,0:T(8,128)}, u32[]{:S(2)}) copy-start(f32[1,64,2048]{2,1,0:T(8,128)} %reduce-scatter.14.cloned.1.call-done) | copy-start | bytes 1572868
  870.0 50.9 %copy-start.44 = (f32[64]{0:T(128)S(1)}, f32[64]{0:T(128)}, u32[]{:S(2)}) copy-start(f32[64]{0:T(128)} %copy-done.42) | copy-start | bytes 772
  (38 other events, 349.6 us)
Sparse Core Ops, SparseCore 0:
  21.3 28.2 all-gather.34
  51.5 27.3 all-gather.36
  80.8 27.8 all-gather.22
  110.7 27.9 all-gather.20
  140.4 30.5 all-gather.38
  182.2 43.7 reduce-scatter.17
  229.2 27.2 all-gather.44
  258.5 42.7 all-gather.46
  303.4 43.3 all-gather.48
  348.8 27.9 all-gather.40
  378.9 43.8 all-gather.42
  436.7 43.8 reduce-scatter.19
  484.8 27.2 all-gather.50
  547.2 20.9 reduce-scatter.21
  570.0 29.6 all-gather.24
  620.6 42.9 reduce-scatter.13
  665.3 42.6 all-gather.28
  710.0 27.9 all-gather.26
  739.8 42.8 all-gather.30
  784.4 44.3 all-gather.32
  831.1 43.8 reduce-scatter.23
  877.4 43.4 reduce-scatter.15
  924.5 33.4 reduce-scatter.27
  961.8 34.1 reduce-scatter.29
  999.9 51.3 reduce-scatter.31
  1055.4 51.3 reduce-scatter.25
  1110.7 86.7 reduce-scatter.33
  1201.6 86.7 reduce-scatter.35
  1292.5 86.7 reduce-scatter.37
where the time goes:
time: 1400 us; the launch traced here: 1390 us
  waiting for transfers between devices  987 us (70%)
  blocking collectives  157 us (11%)
  matrix products  124 us (9%)
  other arithmetic  52.9 us (4%)
  local copies, waits for them, and re-layouts  37.4 us (3%)
  between operations  16.3 us (1%)
    all_gather x6, waiting for transfers between devices, rows_gather(): return lax.all_gather(activations, 'tensor', axis=1, tiled=True)  128 us
    reduce_scatter x5, waiting for transfers between devices, rows_sum(): return lax.psum_scatter(partials, 'tensor', scatter_dimension=1, tiled=True)  122 us
    all_gather x2, waiting for transfers between devices, forward_pass(): lax.all_gather(w_down, ('fsdp', 'context'), axis=1, tiled=True)  92 us
    reduce_scatter x1, waiting for transfers between devices, body(): lax.psum_scatter(grad_down, ('fsdp', 'context'), scatter_dimension=1, til...  90.9 us
    reduce_scatter x1, waiting for transfers between devices, body(): lax.psum_scatter(grad_up, ('fsdp', 'context'), scatter_dimension=0, tiled...  90.9 us
    reduce_scatter x1, waiting for transfers between devices, body(): lax.psum_scatter(grad_gate, ('fsdp', 'context'), scatter_dimension=0, til...  90.7 us
    all_gather x2, waiting for transfers between devices, forward_pass(): lax.all_gather(w_up, ('fsdp', 'context'), axis=0, tiled=True)  83.7 us
    reduce_scatter x1, waiting for transfers between devices, body(): lax.psum_scatter(grad_query, ('fsdp', 'context'), scatter_dimension=0, ti...  55.5 us
  transfers between devices with their start and end apart: 32, of which 27 were waited for; matrix products, arithmetic and copies ran while one was open for 11% of the time, Pallas kernels for 0%

commit v1 on v0

--- a/solution.py
+++ b/solution.py
@@ -6,6 +6,15 @@
 
 EPS = 1e-05
 NEG = -1e30
+settle_ends = lambda point, dim_i: jnp.concatenate(
+    lax.all_to_all(
+        jnp.stack([point for _ in range(lax.axis_size(("fsdp", "context")))]),
+        ("fsdp", "context"),
+        0,
+        0,
+    ),
+    axis=dim_i,
+)
 
 
 def positions_of(segments):
@@ -186,7 +195,7 @@
     middle = hidden_f + branch_one
     gain_two, gate_all, up_all, down_all = (
         lax.all_gather(mlp_gain, ("fsdp", "context"), axis=0, tiled=True),
-        lax.all_gather(w_gate, ("fsdp", "context"), axis=0, tiled=True),
+        settle_ends(w_gate, 0),
         lax.all_gather(w_up, ("fsdp", "context"), axis=0, tiled=True),
         lax.all_gather(w_down, ("fsdp", "context"), axis=1, tiled=True),
     )

time: 1400 us -> 1370 us (0.979)
  waiting for transfers between devices: 987 us -> 869 us
  blocking collectives: 157 us -> 243 us
    all_to_all x0 -> x1, blocking collectives: none -> 88.5 us  [lax.all_to_all(jnp.stack([point for _ in range(lax.axis_size(('fsdp', 'co...]
    all_gather x2, waiting for transfers between devices: 83.7 us -> 0.6 us  [forward_pass(): lax.all_gather(w_up, ('fsdp', 'context'), axis=0, tiled=True)]
    all_to_all x0 -> x1, waiting for transfers between devices: none -> 72.6 us  [lax.all_to_all(jnp.stack([point for _ in range(lax.axis_size(('fsdp', 'co...]
    all_gather x6, waiting for transfers between devices: 128 us -> 74.1 us  [rows_gather(): return lax.all_gather(activations, 'tensor', axis=1, tiled=True)]
    all_gather x2 -> x0, waiting for transfers between devices: 46.7 us -> none  [forward_pass(): lax.all_gather(w_gate, ('fsdp', 'context'), axis=0, tiled=True)]
  transfers between devices with their start and end apart: 32 -> 31, of which waited for: 27 -> 23; matrix products, arithmetic and copies ran while one was open for 11% -> 11% of each run, Pallas kernels for 0% -> 0%
where the time goes in v1:
time: 1370 us; the launch traced here: 1360 us
  waiting for transfers between devices  869 us (63%)
  blocking collectives  243 us (18%)
  matrix products  122 us (9%)
  other arithmetic  54.4 us (4%)
  local copies, waits for them, and re-layouts  41.9 us (3%)
  starting transfers between devices  17.2 us (1%)
  between operations  16.6 us (1%)
    reduce_scatter x5, waiting for transfers between devices, rows_sum(): return lax.psum_scatter(partials, 'tensor', scatter_dimension=1, tiled=True)  123 us
    reduce_scatter x1, waiting for transfers between devices, body(): lax.psum_scatter(grad_gate, ('fsdp', 'context'), scatter_dimension=0, til...  90.9 us
    reduce_scatter x1, waiting for transfers between devices, body(): lax.psum_scatter(grad_up, ('fsdp', 'context'), scatter_dimension=0, tiled...  90.8 us
    reduce_scatter x1, waiting for transfers between devices, body(): lax.psum_scatter(grad_down, ('fsdp', 'context'), scatter_dimension=1, til...  90.7 us
    all_gather x2, waiting for transfers between devices, forward_pass(): lax.all_gather(w_down, ('fsdp', 'context'), axis=1, tiled=True)  90.3 us
    all_to_all x1, blocking collectives, lax.all_to_all(jnp.stack([point for _ in range(lax.axis_size(('fsdp', 'co...  88.5 us
    all_gather x6, waiting for transfers between devices, rows_gather(): return lax.all_gather(activations, 'tensor', axis=1, tiled=True)  74.1 us
    all_to_all x1, waiting for transfers between devices, lax.all_to_all(jnp.stack([point for _ in range(lax.axis_size(('fsdp', 'co...  72.6 us
  transfers between devices with their start and end apart: 31, of which 23 were waited for; matrix products, arithmetic and copies ran while one was open for 11% of the time, Pallas kernels for 0%

profile of v1, /device:TPU:0, one launch (start us, length us, event | category | flops | bytes accessed | tf_op | source)
XLA Modules:
  0.0 1363.5 jit_solution(2128248051814312857)
XLA Ops:
  9.0 10.3 all-gather.2
  23.4 8.8 all-gather
  37.4 9.1 all_gather.85
  46.5 9.6 all_gather.86
  65.9 13.0 all-gather.33.cloned.1.call-done
  83.0 25.7 %all-gather.21.cloned.1.call-done = bf16[2048,512]{1,0:T(8,128)(2,1)} async-done(((bf16[256,512]{1,0:T(8,128)(2,1)}), bf16[2048,512]{1,0:T(8,128)(2,1)}) %all-gather.21.cloned.1.call-update) | async-done | bytes 2097168 | tf_op jit(solution)/shard_map/all_gather | solution.py:160
  114.8 23.8 %all-gather.19.cloned.1.call-done = bf16[1,256,2048]{2,1,0:T(8,128)(2,1)} async-done(((bf16[1,64,2048]{2,1,0:T(8,128)(2,1)}), bf16[1,256,2048]{2,1,0:T(8,128)(2,1)}) %all-gather.19.cloned.1.call-update) | async-done | bytes 1048592 | tf_op jit(solution)/shard_map/all_gather | solution.py:78
  149.1 8.9 all_gather.87
  168.1 8.4 all_to_all.100
  180.9 9.0 all-gather.3
  189.9 35.0 %reduce-scatter.18.cloned.1.call-done = f32[1,64,2048]{2,1,0:T(8,128)} async-done(((f32[1,256,2048]{2,1,0:T(8,128)}), f32[1,64,2048]{2,1,0:T(8,128)}) %reduce-scatter.18.cloned.1.call-update) | async-done | bytes 524304 | tf_op jit(solution)/shard_map/reduce_scatter | solution.py:82
  231.4 88.5 %all_to_all.101 = bf16[8,256,1408]{2,1,0:T(8,128)(2,1)} all-to-all(bf16[8,256,1408]{2,1,0:T(8,128)(2,1)S(1)} %stack.5), channel_id=1, replica_groups=mesh['fsdp'=2,'context'=4,'tensor'=4] {'fsdp','context'}, dimensions={0} | all-to-all | bytes 11534336 | tf_op jit(solution)/shard_map/all_to_all | solution.py:10
  319.9 6.0 fusion.38
  325.9 5.6 fusion.40
  331.5 22.8 %all-gather.37.cloned.1.call-done = bf16[1,256,2048]{2,1,0:T(8,128)(2,1)} async-done(((bf16[1,64,2048]{2,1,0:T(8,128)(2,1)}), bf16[1,256,2048]{2,1,0:T(8,128)(2,1)}) %all-gather.37.cloned.1.call-update) | async-done | bytes 1048592 | tf_op jit(solution)/shard_map/all_gather | solution.py:78
  354.3 45.8 %all-gather.39.cloned.1.call-done = bf16[1408,2048]{1,0:T(8,128)(2,1)} async-done(((bf16[1408,256]{1,0:T(8,128)(2,1)}), bf16[1408,2048]{1,0:T(8,128)(2,1)}) %all-gather.39.cloned.1.call-update) | async-done | bytes 5767184 | tf_op jit(solution)/shard_map/all_gather | solution.py:200
  400.1 6.1 multiply_convert_fusion.1
  412.6 44.0 %reduce-scatter.20.cloned.1.call-done = f32[1,64,2048]{2,1,0:T(8,128)} async-done(((f32[1,256,2048]{2,1,0:T(8,128)}), f32[1,64,2048]{2,1,0:T(8,128)}) %reduce-scatter.20.cloned.1.call-update) | async-done | bytes 524304 | tf_op jit(solution)/shard_map/reduce_scatter | solution.py:82
  460.6 27.4 %all-gather.45.cloned.1.call-done = bf16[1,256,2048]{2,1,0:T(8,128)(2,1)} async-done(((bf16[1,64,2048]{2,1,0:T(8,128)(2,1)}), bf16[1,256,2048]{2,1,0:T(8,128)(2,1)}) %all-gather.45.cloned.1.call-update) | async-done | bytes 1048592 | tf_op jit(solution)/shard_map/all_gather | solution.py:78
  497.7 5.8 all-to-all-done.6
  504.2 5.1 fusion.1
  509.3 4.8 fusion.24
  523.6 10.8 all_gather.74
  534.3 9.9 all_gather.75
  566.9 7.6 all_gather.76
  574.5 6.5 fusion.117
  587.9 8.4 all_to_all.102
  600.6 8.9 all-gather.1
  609.5 34.3 %reduce-scatter.14.cloned.1.call-done = f32[1,64,2048]{2,1,0:T(8,128)} async-done(((f32[1,256,2048]{2,1,0:T(8,128)}), f32[1,64,2048]{2,1,0:T(8,128)}) %reduce-scatter.14.cloned.1.call-update) | async-done | bytes 524304 | tf_op jit(solution)/shard_map/reduce_scatter | solution.py:82
  654.5 9.1 all_to_all.103
  666.5 4.8 all-to-all-start.2
  682.0 72.6 %all-to-all-done.2 = bf16[8,256,1408]{2,1,0:T(8,128)(2,1)} async-done(((bf16[8,256,1408]{2,1,0:T(8,128)(2,1)}), bf16[8,256,1408]{2,1,0:T(8,128)(2,1)}, u32[]{:S(2)}, u32[]{:S(2)}) %all-to-all-start.2) | async-done | bytes 5767200 | tf_op jit(solution)/shard_map/all_to_all | solution.py:10
  754.7 6.0 fusion.56
  761.3 44.6 %all-gather.29.cloned.1.call-done = bf16[1408,2048]{1,0:T(8,128)(2,1)} async-done(((bf16[1408,256]{1,0:T(8,128)(2,1)}), bf16[1408,2048]{1,0:T(8,128)(2,1)}) %all-gather.29.cloned.1.call-update) | async-done | bytes 5767184 | tf_op jit(solution)/shard_map/all_gather | solution.py:200
  805.9 9.5 convolution_bitcast_fusion.1
  824.8 6.1 fusion.36
  832.0 6.1 fusion.34
  839.7 7.3 fusion.42
  853.4 23.9 %all-reduce.2 = (f32[2048]{0:T(1024)S(1)}, f32[2048]{0:T(1024)S(1)}) all-reduce(f32[2048]{0:T(1024)S(1)} %get-tuple-element.99, f32[2048]{0:T(1024)S(1)} %copy-done.45), channel_id=8, replica_groups=mesh['fsdp'=2,'context'=4,'tensor'=4] {'fsdp','context'}, use_global_device_ids=true, to_apply=%region_21.22.clone | all-reduce | flops 4096 | bytes 32768
  877.5 11.4 all-reduce.3
  890.9 6.8 reduce-scatter.16.cloned.1.call-done
  899.6 35.3 %reduce-scatter.28.cloned.1.call-done = f32[256,64]{0,1:T(8,128)} async-done(((f32[2048,64]{0,1:T(8,128)}), f32[256,64]{0,1:T(8,128)}) %reduce-scatter.28.cloned.1.call-update) | async-done | bytes 65552 | tf_op jit(solution)/shard_map/reduce_scatter | solution.py:348
  934.9 38.1 %reduce-scatter.30.cloned.1.call-done = f32[256,64]{0,1:T(8,128)} async-done(((f32[2048,64]{0,1:T(8,128)}), f32[256,64]{0,1:T(8,128)}) %reduce-scatter.30.cloned.1.call-update) | async-done | bytes 65552 | tf_op jit(solution)/shard_map/reduce_scatter | solution.py:349
  973.0 55.3 %reduce-scatter.32.cloned.1.call-done = f32[512,256]{1,0:T(8,128)} async-done(((f32[512,2048]{1,0:T(8,128)}), f32[512,256]{1,0:T(8,128)}) %reduce-scatter.32.cloned.1.call-update) | async-done | bytes 524304 | tf_op jit(solution)/shard_map/reduce_scatter | solution.py:350
  1028.3 55.5 %reduce-scatter.26.cloned.1.call-done = f32[256,512]{1,0:T(8,128)} async-done(((f32[2048,512]{1,0:T(8,128)}), f32[256,512]{1,0:T(8,128)}) %reduce-scatter.26.cloned.1.call-update) | async-done | bytes 524304 | tf_op jit(solution)/shard_map/reduce_scatter | solution.py:347
  1083.8 90.9 %reduce-scatter.34.cloned.1.call-done = f32[256,1408]{1,0:T(8,128)} async-done(((f32[2048,1408]{1,0:T(8,128)}), f32[256,1408]{1,0:T(8,128)}) %reduce-scatter.34.cloned.1.call-update) | async-done | bytes 1441808 | tf_op jit(solution)/shard_map/reduce_scatter | solution.py:289
  1174.7 90.8 %reduce-scatter.36.cloned.1.call-done = f32[256,1408]{1,0:T(8,128)} async-done(((f32[2048,1408]{1,0:T(8,128)}), f32[256,1408]{1,0:T(8,128)}) %reduce-scatter.36.cloned.1.call-update) | async-done | bytes 1441808 | tf_op jit(solution)/shard_map/reduce_scatter | solution.py:290
  1265.5 90.7 %reduce-scatter.38.cloned.1.call-done = f32[1408,256]{1,0:T(8,128)} async-done(((f32[1408,2048]{1,0:T(8,128)}), f32[1408,256]{1,0:T(8,128)}) %reduce-scatter.38.cloned.1.call-update) | async-done | bytes 1441808 | tf_op jit(solution)/shard_map/reduce_scatter | solution.py:291
  (307 shorter events, 172.1 us)
Async XLA Ops:
  7.2 54.0 %all-gather.31.cloned.1.call-start = ((), (), s32[]{:S(2)}) async-start(), calls=%async_computation.29 | async-start | bytes 1310720 | tf_op jit(solution)/shard_map/all_gather | solution.py:78
  21.2 57.7 %all-gather.33.cloned.1.call-start = ((), (), s32[]{:S(2)}) async-start(), calls=%async_computation.30 | async-start | bytes 2359296 | tf_op jit(solution)/shard_map/all_gather | solution.py:160
  21.9 86.8 %all-gather.21.cloned.1.call-start = ((), (), s32[]{:S(2)}) async-start(), calls=%async_computation.22 | async-start | bytes 2359296 | tf_op jit(solution)/shard_map/all_gather | solution.py:160
  22.7 116.0 %all-gather.19.cloned.1.call-start = ((), (), s32[]{:S(2)}) async-start(), calls=%async_computation.21 | async-start | bytes 1310720 | tf_op jit(solution)/shard_map/all_gather | solution.py:78
  35.2 141.9 %all-gather.35.cloned.1.call-start = ((), (), s32[]{:S(2)}) async-start(), calls=%async_computation.31 | async-start | bytes 2359296 | tf_op jit(solution)/shard_map/all_gather | solution.py:163
  56.1 55.6 %copy-start.15 = (bf16[2048,64]{0,1:T(8,128)(2,1)}, bf16[2048,64]{0,1:T(8,128)(2,1)S(1)}, u32[]{:S(2)}) copy-start(bf16[2048,64]{0,1:T(8,128)(2,1)S(1)} %all_gather.86) | copy-start | bytes 786436
  78.9 32.8 %copy-start.3 = (bf16[1,256,2048]{2,1,0:T(8,128)(2,1)S(1)}, bf16[1,256,2048]{2,1,0:T(8,128)(2,1)}, u32[]{:S(2)}) copy-start(bf16[1,256,2048]{2,1,0:T(8,128)(2,1)} %all-gather.31.cloned.1.call-done) | copy-start | bytes 3145732
  145.6 12.4 all-to-all-start.3
  149.0 75.8 %reduce-scatter.18.cloned.1.call-start = ((), (), s32[]{:S(2)}) async-start(), calls=%async_computation.32 | async-start | bytes 2621440 | tf_op jit(solution)/shard_map/reduce_scatter | solution.py:82
  176.5 48.3 %copy-start.2 = (bf16[1,64,2048]{2,1,0:T(8,128)(2,1)S(1)}, bf16[1,64,2048]{2,1,0:T(8,128)(2,1)}, u32[]{:S(2)}) copy-start(bf16[1,64,2048]{2,1,0:T(8,128)(2,1)} %param.13) | copy-start | bytes 786436
  177.0 50.9 %copy-start.11 = (bf16[1,256,4,128]{1,3,2,0:T(8,128)(2,1)}, bf16[1,256,4,128]{1,3,2,0:T(8,128)(2,1)S(1)}, u32[]{:S(2)}) copy-start(bf16[1,256,4,128]{1,3,2,0:T(8,128)(2,1)S(1)} %copy.90) | copy-start | bytes 786436
  177.1 52.4 %copy-start.22 = (bf16[1,64,2048]{2,1,0:T(8,128)(2,1)S(1)}, bf16[1,64,2048]{2,1,0:T(8,128)(2,1)}, u32[]{:S(2)}) copy-start(bf16[1,64,2048]{2,1,0:T(8,128)(2,1)} %param.25) | copy-start | bytes 786436
  180.8 50.2 %copy-start.13 = (bf16[256,1408]{1,0:T(8,128)(2,1)S(1)}, bf16[256,1408]{1,0:T(8,128)(2,1)}, u32[]{:S(2)}) copy-start(bf16[256,1408]{1,0:T(8,128)(2,1)} %param.22) | copy-start | bytes 2162692
  180.8 139.1 %all-gather.41.cloned.1.call-start = ((), (), s32[]{:S(2)}) async-start(), calls=%async_computation.35 | async-start | bytes 1310720 | tf_op jit(solution)/shard_map/all_gather | solution.py:78
  227.9 98.0 %all-gather.43.cloned.1.call-start = ((), (), s32[]{:S(2)}) async-start(), calls=%async_computation.36 | async-start | bytes 6488064 | tf_op jit(solution)/shard_map/all_gather | solution.py:199
  228.7 125.6 %all-gather.37.cloned.1.call-start = ((), (), s32[]{:S(2)}) async-start(), calls=%async_computation.33 | async-start | bytes 1310720 | tf_op jit(solution)/shard_map/all_gather | solution.py:78
  229.5 228.9 %copy-start.48 = (f32[64]{0:T(128)}, f32[64]{0:T(128)S(1)}, u32[]{:S(2)}) copy-start(f32[64]{0:T(128)S(1)} %convert_bitcast_fusion) | copy-start | bytes 772
  230.3 169.8 %all-gather.39.cloned.1.call-start = ((), (), s32[]{:S(2)}) async-start(), calls=%async_computation.34 | async-start | bytes 6488064 | tf_op jit(solution)/shard_map/all_gather | solution.py:200
  230.9 225.6 %reduce-scatter.20.cloned.1.call-start = ((), (), s32[]{:S(2)}) async-start(), calls=%async_computation.37 | async-start | bytes 2621440 | tf_op jit(solution)/shard_map/reduce_scatter | solution.py:82
  409.4 47.2 %copy-start.4 = (f32[1,64,2048]{2,1,0:T(8,128)S(1)}, f32[1,64,2048]{2,1,0:T(8,128)}, u32[]{:S(2)}) copy-start(f32[1,64,2048]{2,1,0:T(8,128)} %reduce-scatter.18.cloned.1.call-done) | copy-start | bytes 1572868
  409.4 49.0 %copy-start.23 = (bf16[1,64,2048]{2,1,0:T(8,128)(2,1)S(1)}, bf16[1,64,2048]{2,1,0:T(8,128)(2,1)}, u32[]{:S(2)}) copy-start(bf16[1,64,2048]{2,1,0:T(8,128)(2,1)} %param.25) | copy-start | bytes 786436
  412.5 75.4 %all-gather.45.cloned.1.call-start = ((), (), s32[]{:S(2)}) async-start(), calls=%async_computation.38 | async-start | bytes 1310720 | tf_op jit(solution)/shard_map/all_gather | solution.py:78
  494.1 9.4 all-to-all-start.6
  497.5 66.3 %reduce-scatter.22.cloned.1.call-start = ((), (), s32[]{:S(2)}) async-start(), calls=%async_computation.39 | async-start | bytes 655360 | tf_op jit(solution)/shard_map/reduce_scatter | solution.py:322
  520.7 35.3 %copy-start.10 = (bf16[1,256,2048]{2,1,0:T(8,128)(2,1)S(1)}, bf16[1,256,2048]{2,1,0:T(8,128)(2,1)}, u32[]{:S(2)}) copy-start(bf16[1,256,2048]{2,1,0:T(8,128)(2,1)} %all-gather.19.cloned.1.call-done) | copy-start | bytes 3145732
  523.0 73.8 %all-gather.23.cloned.1.call-start = ((), (), s32[]{:S(2)}) async-start(), calls=%async_computation.23 | async-start | bytes 2359296 | tf_op jit(solution)/shard_map/all_gather | solution.py:163
  552.0 10.1 all-to-all-start
  556.0 87.8 %reduce-scatter.14.cloned.1.call-start = ((), (), s32[]{:S(2)}) async-start(), calls=%async_computation.24 | async-start | bytes 2621440 | tf_op jit(solution)/shard_map/reduce_scatter | solution.py:82
  596.8 51.2 %copy-start.44 = (f32[1024]{0:T(1024)S(1)}, f32[1024]{0:T(1024)}, u32[]{:S(2)}) copy-start(f32[1024]{0:T(1024)} %copy-done.43) | copy-start | bytes 12292
  596.8 51.2 %copy-start.51 = (f32[32]{0:T(128)S(1)}, f32[32]{0:T(128)}, u32[]{:S(2)}) copy-start(f32[32]{0:T(128)} %copy-done.50) | copy-start | bytes 388
  600.5 154.1 %all-gather.25.cloned.1.call-start = ((), (), s32[]{:S(2)}) async-start(), calls=%async_computation.25 | async-start | bytes 1310720 | tf_op jit(solution)/shard_map/all_gather | solution.py:78
  646.9 114.4 %all-gather.27.cloned.1.call-start = ((), (), s32[]{:S(2)}) async-start(), calls=%async_computation.26 | async-start | bytes 6488064 | tf_op jit(solution)/shard_map/all_gather | solution.py:199
  647.5 158.4 %all-gather.29.cloned.1.call-start = ((), (), s32[]{:S(2)}) async-start(), calls=%async_computation.27 | async-start | bytes 6488064 | tf_op jit(solution)/shard_map/all_gather | solution.py:200
  666.5 88.1 %all-to-all-start.2 = ((bf16[8,256,1408]{2,1,0:T(8,128)(2,1)}), bf16[8,256,1408]{2,1,0:T(8,128)(2,1)}, u32[]{:S(2)}, u32[]{:S(2)}) async-start(bf16[8,256,1408]{2,1,0:T(8,128)(2,1)} %stack.4), calls=%async_computation.3 | async-start | bytes 11534336 | tf_op jit(solution)/shard_map/all_to_all | solution.py:10
  671.4 180.7 %reduce-scatter.24.cloned.1.call-start = ((), (), s32[]{:S(2)}) async-start(), calls=%async_computation.40 | async-start | bytes 2621440 | tf_op jit(solution)/shard_map/reduce_scatter | solution.py:82
  681.7 216.0 %reduce-scatter.16.cloned.1.call-start = ((), (), s32[]{:S(2)}) async-start(), calls=%async_computation.28 | async-start | bytes 2621440 | tf_op jit(solution)/shard_map/reduce_scatter | solution.py:82
  754.7 51.2 %copy-start.53 = (bf16[1,256,2048]{2,1,0:T(8,128)(2,1)S(1)}, bf16[1,256,2048]{2,1,0:T(8,128)(2,1)}, u32[]{:S(2)}) copy-start(bf16[1,256,2048]{2,1,0:T(8,128)(2,1)} %all-gather.25.cloned.1.call-done) | copy-start | bytes 3145732
  760.7 54.7 %copy-start.34 = (bf16[256,32]{0,1:T(8,128)(2,1)S(1)}, bf16[256,32]{0,1:T(8,128)(2,1)}, u32[]{:S(2)}) copy-start(bf16[256,32]{0,1:T(8,128)(2,1)} %get-tuple-element.116) | copy-start | bytes 49156
  815.4 119.5 %reduce-scatter.28.cloned.1.call-start = ((), (), s32[]{:S(2)}) async-start(), calls=%async_computation.42 | async-start | bytes 589824 | tf_op jit(solution)/shard_map/reduce_scatter | solution.py:348
  816.6 156.4 %reduce-scatter.30.cloned.1.call-start = ((), (), s32[]{:S(2)}) async-start(), calls=%async_computation.43 | async-start | bytes 589824 | tf_op jit(solution)/shard_map/reduce_scatter | solution.py:349
  817.8 210.5 %reduce-scatter.32.cloned.1.call-start = ((), (), s32[]{:S(2)}) async-start(), calls=%async_computation.44 | async-start | bytes 4718592 | tf_op jit(solution)/shard_map/reduce_scatter | solution.py:350
  820.5 263.3 %reduce-scatter.26.cloned.1.call-start = ((), (), s32[]{:S(2)}) async-start(), calls=%async_computation.41 | async-start | bytes 4718592 | tf_op jit(solution)/shard_map/reduce_scatter | solution.py:347
  823.3 351.4 %reduce-scatter.34.cloned.1.call-start = ((), (), s32[]{:S(2)}) async-start(), calls=%async_computation.45 | async-start | bytes 12976128 | tf_op jit(solution)/shard_map/reduce_scatter | solution.py:289
  830.9 434.6 %reduce-scatter.36.cloned.1.call-start = ((), (), s32[]{:S(2)}) async-start(), calls=%async_computation.46 | async-start | bytes 12976128 | tf_op jit(solution)/shard_map/reduce_scatter | solution.py:290
  838.1 518.1 %reduce-scatter.38.cloned.1.call-start = ((), (), s32[]{:S(2)}) async-start(), calls=%async_computation.47 | async-start | bytes 12976128 | tf_op jit(solution)/shard_map/reduce_scatter | solution.py:291
  847.0 41.9 %copy-start.19 = (f32[1,64,2048]{2,1,0:T(8,128)S(1)}, f32[1,64,2048]{2,1,0:T(8,128)}, u32[]{:S(2)}) copy-start(f32[1,64,2048]{2,1,0:T(8,128)} %get-tuple-element.106) | copy-start | bytes 1572868
  847.0 50.7 %copy-start.9 = (f32[1,64,2048]{2,1,0:T(8,128)S(1)}, f32[1,64,2048]{2,1,0:T(8,128)}, u32[]{:S(2)}) copy-start(f32[1,64,2048]{2,1,0:T(8,128)} %reduce-scatter.14.cloned.1.call-done) | copy-start | bytes 1572868
  847.0 50.7 %copy-start.49 = (f32[64]{0:T(128)S(1)}, f32[64]{0:T(128)}, u32[]{:S(2)}) copy-start(f32[64]{0:T(128)} %copy-done.48) | copy-start | bytes 772
  (40 other events, 316.4 us)
Sparse Core Ops, SparseCore 0:
  21.3 28.2 all-gather.30
  51.5 27.3 all-gather.32
  80.8 27.8 all-gather.20
  110.7 27.9 all-gather.18
  140.4 30.4 all-gather.34
  180.9 43.8 reduce-scatter.17
  228.1 27.2 all-gather.40
  257.4 68.2 all-gather.42
  328.0 26.3 all-gather.36
  356.2 43.8 all-gather.38
  412.6 43.8 reduce-scatter.19
  460.7 27.2 all-gather.44
  523.1 20.3 reduce-scatter.21
  545.4 30.3 all-gather.22
  600.7 43.0 reduce-scatter.13
  647.0 27.2 all-gather.24
  676.0 85.1 all-gather.26
  763.0 42.7 all-gather.28
  808.1 43.8 reduce-scatter.23
  854.3 43.4 reduce-scatter.15
  901.4 33.4 reduce-scatter.27
  938.8 34.1 reduce-scatter.29
  977.0 51.2 reduce-scatter.31
  1032.4 51.3 reduce-scatter.25
  1087.9 86.7 reduce-scatter.33
  1178.7 86.7 reduce-scatter.35
  1269.4 86.7 reduce-scatter.37
